TPU v7x, 32 devices: a whole 2x2x4 slice. The times are simulated.
32 devices in a mesh: ctx: 16 (over z, x, core), head: 2 (over y).
Axes of the slice: x: 2, y: 2, z: 4, core: 2. Of those that a mesh axis runs over, the one named last changes fastest.
Arguments:
- q_latent: bfloat16 [2048, 1536], P(('ctx', 'head')), may hold values from -320 to 320
- q_gain: float32 [1536], replicated, may hold values from 0.5 to 8
- kv_cache: bfloat16 [2048, 576], P(('ctx', 'head')), may hold values from -320 to 320
- kv_gain: float32 [512], replicated, may hold values from 0.5 to 8
- w_query: bfloat16 [1536, 12288], P(None, 'head'), may hold values from -0.15625 to 0.15625
- w_kv: bfloat16 [512, 16384], P(None, 'head'), may hold values from -0.25 to 0.25
- doc_lengths: int32 [3], replicated, may hold values from 1 to 1024, 2048 in all
Outputs:
- attn_out: bfloat16 [2048, 8192], P('ctx', 'head')
Inputs may be any that keep to these rules, and one draw needn't show every extreme that they name: `doc_lengths`: 3 documents, lengths in order summing to 2048; the longest has exactly 1024 tokens.
All inputs are finite; a program needn't handle non-finite values.
Results may differ from a plain program's by a relative error of at most 0.0075.
The roundings to bfloat16 on the way count: a program that leaves them out, or rounds other values in their place, can miss the bound.
Values may be sent and summed in bfloat16 or wider, within the bound.
A program may use at most 192 MiB of HBM per device.

v0:
```python
import math

import jax
import jax.numpy as jnp
from jax import lax
from jax.sharding import PartitionSpec as P

KL = 512
RD = 64
ND = 128
VD = 128


epsilon = 1e-06


def rms_scale(rows, gain):
    values = rows.astype(jnp.float32)
    return values * lax.rsqrt(jnp.mean(values * values, axis=-1, keepdims=True) + epsilon) * gain


def doc_tables(doc_lengths, positions):
    doc_ends = jnp.cumsum(doc_lengths)
    passed = positions[:, None] >= doc_ends[None, :]
    doc_index = jnp.sum(passed.astype(jnp.int32), axis=1)
    doc_start = jnp.sum(jnp.where(passed, doc_lengths[None, :], 0), axis=1)
    return (doc_index, doc_start)


def rotate_pairs(values, offsets):
    half_width = values.shape[-1] // 2
    freq_index = jnp.arange(half_width, dtype=jnp.float32)
    frequency = jnp.exp(freq_index * (-2.0 * math.log(10000.0) / values.shape[-1]))
    angles = offsets.astype(jnp.float32)[:, None] * frequency[None, :]
    cosine = jnp.cos(angles)[:, None, :]
    sine_part = jnp.sin(angles)[:, None, :]
    lower_half = values[..., :half_width]
    upper_half = values[..., half_width:]
    return jnp.concatenate(
        [
            lower_half * cosine - upper_half * sine_part,
            upper_half * cosine + lower_half * sine_part,
        ],
        axis=-1,
    )


def project_queries(latent_rows, q_gain, w_query, offsets, nope_width, rope_width):
    normed = rms_scale(latent_rows, q_gain).astype(jnp.bfloat16)
    projected = jnp.dot(normed, w_query, preferred_element_type=jnp.float32)
    head_count = w_query.shape[1] // (nope_width + rope_width)
    projected = projected.reshape(latent_rows.shape[0], head_count, nope_width + rope_width)
    rotated = rotate_pairs(projected[..., nope_width:], offsets)
    return jnp.concatenate([projected[..., :nope_width], rotated], axis=-1).astype(jnp.bfloat16)


def body(q_latent, q_gain, kv_cache, kv_gain, w_query, w_kv, doc_lengths):
    tok_dev = q_latent.shape[0] * lax.axis_size("head")
    heads_here = w_query.shape[1] // (ND + RD)
    ctx_first = lax.axis_index("ctx") * tok_dev
    score_scale = 1.0 / math.sqrt(ND + RD)
    block_rows = lax.all_gather(q_latent, "head", axis=0, tiled=True)
    positions = ctx_first + jnp.arange(block_rows.shape[0], dtype=jnp.int32)
    unused_index, doc_start = doc_tables(doc_lengths, positions)
    made = project_queries(block_rows, q_gain, w_query, positions - doc_start, ND, RD)
    queries = made.reshape(block_rows.shape[0], heads_here * (ND + RD))
    queries = queries.reshape(tok_dev, heads_here, ND + RD)
    q_nope = queries[..., :ND]
    q_rope = queries[..., ND:]
    block_rows = lax.all_gather(kv_cache, "head", axis=0, tiled=True)
    normed = rms_scale(block_rows[:, :KL], kv_gain).astype(jnp.bfloat16)
    payload = jnp.concatenate([normed, block_rows[:, KL:]], axis=1)
    query_pos = ctx_first + jnp.arange(tok_dev, dtype=jnp.int32)
    query_doc, unused_start = doc_tables(doc_lengths, query_pos)
    block_rows = lax.all_gather(payload, "ctx", axis=0, tiled=True)
    running_max = jnp.full((tok_dev, heads_here), -1e30, jnp.float32)
    rows_here = block_rows.shape[0]
    expanded = jnp.dot(block_rows[:, :KL], w_kv, preferred_element_type=jnp.float32).astype(
        jnp.bfloat16
    )
    expanded = expanded.reshape(rows_here, heads_here, ND + VD)
    key_rope = block_rows[:, block_rows.shape[1] - RD :]
    key_pos = jnp.arange(rows_here, dtype=jnp.int32)
    key_doc, unused_offset = doc_tables(doc_lengths, key_pos)
    allowed = (key_pos[None, :] <= query_pos[:, None]) & (key_doc[None, :] == query_doc[:, None])
    scores = jnp.einsum(
        "qhd,khd->qhk", q_nope, expanded[..., :ND], preferred_element_type=jnp.float32
    )
    scores = scores + jnp.einsum(
        "qhr,kr->qhk", q_rope, key_rope, preferred_element_type=jnp.float32
    )
    scores = scores * score_scale
    masked = jnp.where(allowed[:, None, :], scores, -1e30)
    new_max = jnp.maximum(running_max, jnp.max(masked, axis=-1))
    weights = jnp.where(allowed[:, None, :], jnp.exp(scores - new_max[..., None]), 0.0)
    row_total = jnp.sum(weights, axis=-1)
    mixed = jnp.einsum(
        "qhk,khv->qhv",
        weights.astype(jnp.bfloat16),
        expanded[..., ND:],
        preferred_element_type=jnp.float32,
    )
    weighted = mixed
    running_max, row_total, weighted = (new_max, row_total, weighted)
    outputs = weighted / row_total[..., None]
    return outputs.reshape(tok_dev, heads_here * VD).astype(jnp.bfloat16)


def solution(mesh):
    placed = (
        P(("ctx", "head"), None),
        P(),
        P(("ctx", "head"), None),
        P(),
        P(None, "head"),
        P(None, "head"),
        P(),
    )
    return jax.shard_map(
        body, mesh=mesh, in_specs=placed, out_specs=P("ctx", "head"), check_vma=False
    )
```

profile of v0, /device:TPU:25, one launch (start us, length us, event | category | flops | bytes accessed | tf_op | source)
XLA Modules:
  0.0 219.7 jit_solution(5932113530830580022)
XLA Ops:
  6.5 0.0 all-gather.2.cloned.1.call-start
  6.5 4.2 %all_gather.9 = bf16[128,576]{1,0:T(8,128)(2,1)S(1)} all-gather(bf16[64,576]{1,0:T(8,128)(2,1)} %param.9), channel_id=1, replica_groups=mesh['ctx'=16,'head'=2] {'head'}, dimensions={0}, use_global_device_ids=true | all-gather | bytes 221184 | tf_op jit(solution)/shard_map/all_gather | solution.py:70
  10.7 0.1 copy.56
  10.8 0.1 fusion.28
  10.9 0.1 copy.57
  11.0 0.8 fusion.30
  11.9 0.7 pad_maximum_fusion
  12.5 0.0 all-gather.2.cloned.1.call-update
  12.6 0.8 reduce-window.8
  13.4 5.4 %all_gather.11 = bf16[128,1536]{1,0:T(8,128)(2,1)S(1)} all-gather(bf16[64,1536]{1,0:T(8,128)(2,1)} %param.7), channel_id=1, replica_groups=mesh['ctx'=16,'head'=2] {'head'}, dimensions={0}, use_global_device_ids=true | all-gather | bytes 589824 | tf_op jit(solution)/shard_map/all_gather | solution.py:62
  18.8 0.1 convert_reduce_fusion
  18.9 0.7 fusion.31
  19.6 0.2 fusion.18
  19.8 0.1 multiply_cosine_fusion
  20.0 11.4 %fusion.24 = f32[128,6144]{0,1:T(8,128)S(1)} fusion(bf16[1536,6144]{1,0:T(8,128)(2,1)} %param.11, bf16[128,1536]{1,0:T(8,128)(2,1)S(1)} %all_gather.11, f32[1536]{0:T(1024)} %param.8, f32[128]{0:T(128)S(1)} %add_rsqrt_fusion), kind=kOutput, calls=%fused_computation.30 | convolution fusion | flops 2416705536 | bytes 22419968 | tf_op jit(solution)/shard_map/dot_general | solution.py:50
  31.4 0.9 subtract_convert_fusion
  32.3 0.3 fusion.17
  32.7 23.1 %all-gather.2.cloned.1.call-done = bf16[2048,576]{0,1:T(8,128)(2,1)} async-done(((bf16[128,576]{0,1:T(8,128)(2,1)}), bf16[2048,576]{0,1:T(8,128)(2,1)}) %all-gather.2.cloned.1.call-update) | async-done | bytes 2359312 | tf_op jit(solution)/shard_map/all_gather | solution.py:75
  55.8 25.0 %convolution_convert_fusion = bf16[2048,8192]{1,0:T(8,128)(2,1)} fusion(bf16[512,8192]{1,0:T(8,128)(2,1)} %param.12, bf16[2048,576]{0,1:T(8,128)(2,1)} %all-gather.2.cloned.1.call-done), kind=kOutput, calls=%fused_computation.4 | convolution fusion | flops 17196646400 | bytes 44040192 | tf_op jit(solution)/shard_map/dot_general | solution.py:78
  80.8 23.1 %copy.60 = bf16[256,8,32,256]{3,2,1,0:T(8,128)(2,1)} copy(bf16[256,8,32,256]{3,1,2,0:T(8,128)(2,1)} %bitcast.22) | data formatting | bytes 67108864
  103.8 24.1 %fusion.35 = (bf16[2048,32,128]{2,1,0:T(8,128)(2,1)}, bf16[2048,32,128]{2,1,0:T(8,128)(2,1)}) fusion(bf16[2048,32,256]{2,1,0:T(8,128)(2,1)} %bitcast.21), kind=kLoop, calls=%fused_computation.56 | loop fusion | bytes 67108864 | tf_op jit(solution)/shard_map/slice | solution.py:100
  128.0 17.5 %fusion.5 = f32[32,2048,128]{2,1,0:T(8,128)} fusion(bf16[2048,32,128]{2,1,0:T(8,128)(2,1)} %get-tuple-element.8, f32[128,32,192]{0,2,1:T(8,128)S(1)} %bitcast.24), kind=kOutput, calls=%fused_computation.8 | convolution fusion | flops 2147483648 | bytes 51380224 | tf_op jit(solution)/shard_map/qhd,khd->qhk/dot_general | solution.py:86
  145.5 24.8 %select_reduce_fusion = (f32[128,32]{0,1:T(8,128)S(1)}, f32[128,32,2048]{0,2,1:T(8,128)}) fusion(pred[128,2048]{0,1:T(8,128)(4,1)S(1)} %fusion.17, bf16[2048,576]{0,1:T(8,128)(2,1)} %all-gather.2.cloned.1.call-done, bf16[128,32,32]{0,2,1:T(8,128)(2,1)} %get-tuple-element.10, bf16[128,32,32]{0,2,1:T(8,128)(2,1)} %get-tuple-element.9, f32[32,2048,128]{2,1,0:T(8,128)} %fusion.5), kind=kOutput, calls=%fused_computation.3 | convolution fusion | flops 1108340736 | bytes 68173824 | tf_op jit(solution)/shard_map/qhr,kr->qhk/dot_general | solution.py:89
  170.3 13.7 %fusion.1 = f32[128,32]{0,1:T(8,128)S(1)} fusion(f32[128,32,2048]{0,2,1:T(8,128)} %get-tuple-element.14, f32[128,32]{0,1:T(8,128)S(1)} %broadcast_maximum_fusion, pred[128,2048]{0,1:T(8,128)(4,1)S(1)} %fusion.17), kind=kLoop, calls=%fused_computation.5 | loop fusion | flops 25161728 | bytes 33849344 | tf_op jit(solution)/shard_map/reduce_sum | solution.py:96
  184.0 27.5 %fusion.12 = bf16[128,32,128]{0,2,1:T(8,128)(2,1)S(1)} fusion(f32[128,32,2048]{0,2,1:T(8,128)} %get-tuple-element.14, f32[128,32]{0,1:T(8,128)S(1)} %broadcast_maximum_fusion, pred[128,2048]{0,1:T(8,128)(4,1)S(1)} %fusion.17, bf16[2048,32,128]{2,1,0:T(8,128)(2,1)} %get-tuple-element.7, f32[128,32]{0,1:T(8,128)S(1)} %fusion.1), kind=kOutput, calls=%fused_computation.17 | convolution fusion | flops 2173698048 | bytes 51675136 | tf_op jit(solution)/shard_map/qhk,khv->qhv/dot_general | solution.py:97
  211.6 1.3 copy.51
  (8 shorter events, 0.0 us)
Async XLA Ops:
  6.5 49.2 %all-gather.2.cloned.1.call-start = ((), (), s32[]{:S(2)}) async-start(), calls=%async_computation | async-start | bytes 2506752 | tf_op jit(solution)/shard_map/all_gather | solution.py:75
Sparse Core Ops, SparseCore 0:
  12.7 43.0 all-gather.1
where the time goes:
time: 223 us; the launch traced here: 220 us
  matrix products  106 us (48%)
  local copies, waits for them, and re-layouts  48.7 us (22%)
  waiting for transfers between devices  23.1 us (10%)
  other arithmetic  18.6 us (8%)
  between operations  13.5 us (6%)
  blocking collectives  9.54 us (4%)
    dot_general x1, matrix products, body(): jnp.einsum('qhk,khv->qhv', weights.astype(jnp.bfloat16), expanded[..., ND...  27.5 us
    dot_general x1, matrix products, body(): jnp.dot(block_rows[:, :KL], w_kv, preferred_element_type=jnp.float32)  25 us
    dot_general x1, matrix products, body(): jnp.einsum('qhr,kr->qhk', q_rope, key_rope, preferred_element_type=jnp.fl...  24.8 us
    slice x1, local copies, waits for them, and re-layouts, body(): expanded[..., ND:]  24.1 us
    unnamed x3, local copies, waits for them, and re-layouts  23.3 us
    all_gather x1, waiting for transfers between devices, body(): block_rows = lax.all_gather(payload, 'ctx', axis=0, tiled=True)  23.1 us
    dot_general x1, matrix products, body(): jnp.einsum('qhd,khd->qhk', q_nope, expanded[..., :ND], preferred_element_...  17.5 us
    reduce_sum x1, other arithmetic, body(): row_total = jnp.sum(weights, axis=-1)  13.7 us
  transfers between devices with their start and end apart: 1, of which 1 were waited for; matrix products, arithmetic and copies ran while one was open for 7% of the time, Pallas kernels for 0%

commit v1 on v0

v1 whole, which is shorter than its diff:
```python
import functools
import math

import jax
import jax.numpy as jnp
from jax import lax
from jax.experimental import pallas as pl
from jax.experimental.pallas import tpu as pltpu
from jax.sharding import PartitionSpec as P

KL = 512
RD = 64
ND = 128
VD = 128
MESH = pl.DeviceIdType.MESH

epsilon = 1e-06


def gather_kernel(nc, nh, q_ref, kv_ref, qall_ref, win_ref, q_send, q_recv, a_send, a_recv, b_send, b_recv, c_send, c_recv):
    c = lax.axis_index("ctx")
    h = lax.axis_index("head")
    rows = kv_ref.shape[0]
    back = nc // 2
    half = back // 2
    par = lax.rem(c, 2)
    other = c + 1 - 2 * par
    head_of = [lax.rem(h + k, nh) for k in range(nh)]

    def part(slot, head):
        return win_ref.at[slot, pl.ds(pl.multiple_of(head * rows, rows), rows)]

    def qpart(head):
        return qall_ref.at[pl.ds(pl.multiple_of(head * rows, rows), rows)]

    def remote(src, dst, send, recv, ctx, head):
        return pltpu.make_async_remote_copy(
            src_ref=src, dst_ref=dst, send_sem=send, recv_sem=recv, device_id=(ctx, head), device_id_type=MESH
        )

    barrier = pltpu.get_barrier_semaphore()

    def greet(ctx, head):
        pl.semaphore_signal(barrier, inc=1, device_id=(ctx, head), device_id_type=MESH)

    for k in range(1, nh):
        greet(c, head_of[k])
    greet(other, h)
    for j in range(1, nc // 2):
        greet(lax.rem(c + 2 * j, nc), h)
    pl.semaphore_wait(barrier, nh + nc // 2 - 1)

    def q_copy(k):
        return remote(q_ref, qpart(h), q_send.at[k - 1], q_recv.at[k - 1], c, head_of[k])

    def a_copy(j):
        return remote(kv_ref, part(back - 2 * j, h), a_send.at[j - 1], a_recv.at[j - 1], c + 2 * j, h)

    def b_copy(j, k):
        src = kv_ref if j == 0 else part(back - 2 * j, h)
        return remote(src, part(back - 2 * j, h), b_send.at[j, k - 1], b_recv.at[j, k - 1], c, head_of[k])

    def c_copy(t, k, src=None):
        head = head_of[0] if k == 0 else head_of[nh - k]
        src = part(back - 2 * t - 2 * par, head) if src is None else src
        return remote(src, part(back - 2 * t - 1, head), c_send.at[t, k], c_recv.at[t, k], other, h)

    for j in range(1, half + 1):
        pl.when(c + 2 * j < nc)(lambda j=j: a_copy(j).start())
    for k in range(1, nh):
        b_copy(0, k).start()
        q_copy(k).start()

    @pl.when(par == 0)
    def _():
        c_copy(0, 0, kv_ref).start()

    win_ref[back, pl.ds(pl.multiple_of(h * rows, rows), rows)] = kv_ref[...]
    qall_ref[pl.ds(pl.multiple_of(h * rows, rows), rows)] = q_ref[...]
    for slot in range(back):
        @pl.when(c - back + slot < 0)
        def _(slot=slot):
            win_ref[slot] = jnp.zeros(win_ref.shape[1:], win_ref.dtype)

    def forward(j, k):
        if j < half:
            @pl.when(par == 0)
            def _():
                c_copy(j, k).start()
        if j > 0:
            @pl.when(par == 1)
            def _():
                c_copy(j - 1, k).start()

    for k in range(1, nh):
        b_copy(0, k).wait_recv()
        forward(0, k)
    for j in range(1, half + 1):
        @pl.when(c - 2 * j >= 0)
        def _(j=j):
            a_copy(j).wait_recv()
            for k in range(1, nh):
                b_copy(j, k).start()
            forward(j, 0)
    for j in range(1, half + 1):
        @pl.when(c - 2 * j >= 0)
        def _(j=j):
            for k in range(1, nh):
                b_copy(j, k).wait_recv()
                forward(j, k)
    for k in range(1, nh):
        q_copy(k).wait_recv()
    for t in range(half):
        @pl.when(c - 2 * t - 1 >= 0)
        def _(t=t):
            for k in range(nh):
                c_copy(t, k).wait_recv()
    for k in range(1, nh):
        q_copy(k).wait_send()
        b_copy(0, k).wait_send()
    for j in range(1, half + 1):
        pl.when(c + 2 * j < nc)(lambda j=j: a_copy(j).wait_send())

        @pl.when(c - 2 * j >= 0)
        def _(j=j):
            for k in range(1, nh):
                b_copy(j, k).wait_send()
    for t in range(half):
        @pl.when(c - 2 * t - 2 * par >= 0)
        def _(t=t):
            for k in range(nh):
                c_copy(t, k).wait_send()


def gather(q_latent, kv_cache, nc, nh):
    rows, ql = q_latent.shape
    width = kv_cache.shape[1]
    back = nc // 2
    half = back // 2
    peers = max(nh - 1, 1)
    dma = pltpu.SemaphoreType.DMA
    vmem = pl.BlockSpec(memory_space=pltpu.VMEM)
    return pl.pallas_call(
        functools.partial(gather_kernel, nc, nh),
        out_shape=(
            jax.ShapeDtypeStruct((nh * rows, ql), q_latent.dtype),
            jax.ShapeDtypeStruct((back + 1, nh * rows, width), kv_cache.dtype),
        ),
        in_specs=[vmem, vmem],
        out_specs=(vmem, vmem),
        scratch_shapes=[
            dma((peers,)), dma((peers,)), dma((half,)), dma((half,)),
            dma((half + 1, peers)), dma((half + 1, peers)), dma((half, nh)), dma((half, nh)),
        ],
        compiler_params=pltpu.CompilerParams(collective_id=0, has_side_effects=True),
        name="gather",
    )(q_latent, kv_cache)


def normed(values, gain):
    values = values.astype(jnp.float32)
    mean = jnp.mean(values * values, axis=-1, keepdims=True)
    return (values * lax.rsqrt(mean + epsilon) * gain).astype(jnp.bfloat16)


def attend_kernel(heads, first_ref, len_ref, q_ref, qg_ref, win_ref, kvg_ref, wq_ref, wkv_ref, out_ref, qn, kvn, kr, bias, cos, sin):
    tok = q_ref.shape[0]
    keys = win_ref.shape[0]
    docs = len_ref.shape[0]

    @pl.when(pl.program_id(0) == 0)
    def _():
        first = first_ref[0]
        qn[...] = normed(q_ref[...], qg_ref[...])
        kvn[...] = normed(win_ref[:, :KL], kvg_ref[...])
        kr[...] = win_ref[:, KL:]

        def start_of(pos):
            start = jnp.zeros_like(pos)
            end = jnp.int32(0)
            for d in range(docs):
                end = end + len_ref[d]
                start = start + jnp.where(pos >= end, len_ref[d], 0)
            return start

        qpos = first + lax.broadcasted_iota(jnp.int32, (tok, keys), 0)
        kpos = first - (keys - tok) + lax.broadcasted_iota(jnp.int32, (tok, keys), 1)
        allowed = (kpos <= qpos) & (kpos >= start_of(qpos))
        bias[...] = jnp.where(allowed, 0.0, -1e30)
        pos = first + lax.broadcasted_iota(jnp.int32, (tok, RD), 0)
        lane = lax.broadcasted_iota(jnp.int32, (tok, RD), 1)
        freq_index = jnp.where(lane < RD // 2, lane, lane - RD // 2).astype(jnp.float32)
        frequency = jnp.exp(freq_index * (-2.0 * math.log(10000.0) / RD))
        angles = (pos - start_of(pos)).astype(jnp.float32) * frequency
        cos[...] = jnp.cos(angles)
        sine = jnp.sin(angles)
        sin[...] = jnp.where(lane < RD // 2, -sine, sine)

    scale = math.log2(math.e) / math.sqrt(ND + RD)
    made = jnp.dot(qn[...], wq_ref[...], preferred_element_type=jnp.float32)
    for n in range(heads):
        at = n * (ND + RD)
        turn = made[:, at + ND : at + ND + RD]
        swapped = jnp.concatenate([turn[:, RD // 2 :], turn[:, : RD // 2]], axis=1)
        turn = turn * cos[...] + swapped * sin[...]
        query = jnp.concatenate([made[:, at : at + ND], turn], axis=1).astype(jnp.bfloat16)
        at = n * (ND + VD)
        expanded = jnp.dot(
            kvn[...], wkv_ref[:, at : at + ND + VD], preferred_element_type=jnp.float32
        ).astype(jnp.bfloat16)
        key = jnp.concatenate([expanded[:, :ND], kr[...]], axis=1)
        scores = lax.dot_general(query, key, (((1,), (1,)), ((), ())), preferred_element_type=jnp.float32)
        scores = scores + bias[...]
        top = jnp.max(scores, axis=1, keepdims=True)
        weights = jnp.exp2((scores - top) * scale)
        total = jnp.sum(weights, axis=1, keepdims=True)
        mixed = jnp.dot(weights.astype(jnp.bfloat16), expanded[:, ND:], preferred_element_type=jnp.float32)
        out_ref[:, n * VD : (n + 1) * VD] = (mixed / total).astype(jnp.bfloat16)


def attend(first, doc_lengths, q_rows, q_gain, window, kv_gain, w_query, w_kv, heads):
    tok, ql = q_rows.shape
    keys, width = window.shape
    all_heads = w_query.shape[1] // (ND + RD)
    whole = lambda shape: pl.BlockSpec(shape, lambda i, *refs: (0, 0))
    return pl.pallas_call(
        functools.partial(attend_kernel, heads),
        out_shape=jax.ShapeDtypeStruct((tok, all_heads * VD), jnp.bfloat16),
        grid_spec=pltpu.PrefetchScalarGridSpec(
            num_scalar_prefetch=2,
            grid=(all_heads // heads,),
            in_specs=[
                whole((tok, ql)),
                whole((1, ql)),
                whole((keys, width)),
                whole((1, KL)),
                pl.BlockSpec((ql, heads * (ND + RD)), lambda i, *refs: (0, i)),
                pl.BlockSpec((KL, heads * (ND + VD)), lambda i, *refs: (0, i)),
            ],
            out_specs=pl.BlockSpec((tok, heads * VD), lambda i, *refs: (0, i)),
            scratch_shapes=[
                pltpu.VMEM((tok, ql), jnp.bfloat16),
                pltpu.VMEM((keys, KL), jnp.bfloat16),
                pltpu.VMEM((keys, RD), jnp.bfloat16),
                pltpu.VMEM((tok, keys), jnp.float32),
                pltpu.VMEM((tok, RD), jnp.float32),
                pltpu.VMEM((tok, RD), jnp.float32),
            ],
        ),
        compiler_params=pltpu.CompilerParams(
            dimension_semantics=("arbitrary",), vmem_limit_bytes=60 * 2**20
        ),
        name="attend",
    )(first, doc_lengths, q_rows, q_gain, window, kv_gain, w_query, w_kv)


def solution(mesh):
    nc, nh = mesh.shape["ctx"], mesh.shape["head"]

    def body(q_latent, q_gain, kv_cache, kv_gain, w_query, w_kv, doc_lengths):
        q_rows, window = gather(q_latent, kv_cache, nc, nh)
        first = (lax.axis_index("ctx") * q_rows.shape[0]).astype(jnp.int32).reshape(1)
        window = window.reshape(-1, window.shape[-1])
        return attend(first, doc_lengths, q_rows, q_gain[None], window, kv_gain[None], w_query, w_kv, 4)

    placed = (
        P(("ctx", "head"), None),
        P(),
        P(("ctx", "head"), None),
        P(),
        P(None, "head"),
        P(None, "head"),
        P(),
    )
    return jax.shard_map(body, mesh=mesh, in_specs=placed, out_specs=P("ctx", "head"), check_vma=False)
```

time: 223 us -> 67.4 us (0.30); the launches traced: 220 us -> 67.2 us
  matrix products: 106 us -> 0 us
  Pallas kernels: 0 us -> 65.9 us
  local copies, waits for them, and re-layouts: 48.7 us -> 1.29 us
  waiting for transfers between devices: 23.1 us -> 0 us
  other arithmetic: 18.6 us -> 0 us
  between operations: 13.5 us -> 0.01 us
  blocking collectives: 9.54 us -> 0 us
    dot_general x5 -> x0, matrix products: 106 us -> none  [the longest x1 27.5 us: body(): jnp.einsum('qhk,khv->qhv', weights.astype(jnp.bfloat16), expanded[..., ND...]
    pallas_call x0 -> x2, Pallas kernels: none -> 65.9 us  [the longest x1 44 us: attend(): pl.pallas_call(functools.partial(attend_kernel, heads), out_shape=jax.Sha...]
    slice x3 -> x0, local copies, waits for them, and re-layouts: 24.1 us -> none  [the longest x1 24.1 us: body(): expanded[..., ND:]]
    unnamed x3 -> x0, local copies, waits for them, and re-layouts: 23.3 us -> none
    all_gather x1 -> x0, waiting for transfers between devices: 23.1 us -> none  [body(): block_rows = lax.all_gather(payload, 'ctx', axis=0, tiled=True)]
    reduce_sum x5 -> x0, other arithmetic: 14.8 us -> none  [the longest x1 13.7 us: body(): row_total = jnp.sum(weights, axis=-1)]
    all_gather x2 -> x0, blocking collectives: 9.54 us -> none  [the longest x1 5.38 us: body(): block_rows = lax.all_gather(q_latent, 'head', axis=0, tiled=True)]
  transfers between devices with their start and end apart: 1 -> 0, of which waited for: 1 -> 0; matrix products, arithmetic and copies ran while one was open for 7% -> 0% of each run, Pallas kernels for 0% -> 0%
where the time goes in v1:
time: 67.4 us; the launch traced here: 67.2 us
  Pallas kernels  65.9 us (98%)
  local copies, waits for them, and re-layouts  1.29 us (2%)
    pallas_call x1, Pallas kernels, attend(): pl.pallas_call(functools.partial(attend_kernel, heads), out_shape=jax.Sha...  44 us
    pallas_call x1, Pallas kernels, gather(): pl.pallas_call(functools.partial(gather_kernel, nc, nh), out_shape=(jax.S...  21.9 us

profile of v1, /device:TPU:25, one launch (start us, length us, event | category | flops | bytes accessed | tf_op | source)
XLA Modules:
  0.0 67.2 jit_solution(3990216403603344349)
XLA Ops:
  0.0 1.3 %broadcast_in_dim.6.qg_ref = f32[1,1536]{1,0:T(1,128)} reshape(f32[1536]{0:T(1024)} %param.8) | data formatting | bytes 12288 | tf_op jit(solution)/shard_map/broadcast_in_dim | solution.py:264
  1.3 21.9 %gather.1 = (bf16[128,1536]{1,0:T(8,128)(2,1)}, bf16[9,128,576]{2,1,0:T(8,128)(2,1)}) custom-call(bf16[64,1536]{1,0:T(8,128)(2,1)} %q_ref.1, bf16[64,576]{1,0:T(8,128)(2,1)} %kv_ref.1), custom_call_target="tpu_custom_call" | custom-call | tf_op jit(solution)/shard_map/gather/pallas_call | solution.py:143
  23.2 44.0 %attend.1 = bf16[128,4096]{1,0:T(8,128)(2,1)} custom-call(s32[1]{0:T(128)} %bitcast.first_ref, s32[3]{0:T(128)} %len_ref.1, bf16[128,1536]{1,0:T(8,128)(2,1)} %get-tuple-element.7.q_ref, f32[1,1536]{1,0:T(1,128)} %broadcast_in_dim.6.qg_ref, bf16[1152,576]{1,0:T(8,128)(2,1)} %bitcast.3, f32[1,512]{1,0:T(1,128)} %bitcast.4, bf16[1536,6144]{1,0:T(8,128)(2,1)} %wq_ref.1, ...), custom_call_target="tpu_custom_call" | custom-call | tf_op jit(solution)/shard_map/attend/pallas_call | solution.py:226

commit v2 on v1

--- a/solution.py
+++ b/solution.py
@@ -171,7 +171,7 @@
     @pl.when(pl.program_id(0) == 0)
     def _():
         first = first_ref[0]
-        qn[...] = normed(q_ref[...], qg_ref[...])
+        qn[...] = normed(q_ref[...], qg_ref[...][None])
         kvn[...] = normed(win_ref[:, :KL], kvg_ref[...])
         kr[...] = win_ref[:, KL:]
 
@@ -198,23 +198,32 @@
 
     scale = math.log2(math.e) / math.sqrt(ND + RD)
     made = jnp.dot(qn[...], wq_ref[...], preferred_element_type=jnp.float32)
-    for n in range(heads):
+
+    def query_of(n):
         at = n * (ND + RD)
         turn = made[:, at + ND : at + ND + RD]
         swapped = jnp.concatenate([turn[:, RD // 2 :], turn[:, : RD // 2]], axis=1)
         turn = turn * cos[...] + swapped * sin[...]
-        query = jnp.concatenate([made[:, at : at + ND], turn], axis=1).astype(jnp.bfloat16)
+        return jnp.concatenate([made[:, at : at + ND], turn], axis=1).astype(jnp.bfloat16)
+
+    def expand(n):
         at = n * (ND + VD)
-        expanded = jnp.dot(
+        return jnp.dot(
             kvn[...], wkv_ref[:, at : at + ND + VD], preferred_element_type=jnp.float32
         ).astype(jnp.bfloat16)
+
+    def score(query, expanded):
         key = jnp.concatenate([expanded[:, :ND], kr[...]], axis=1)
         scores = lax.dot_general(query, key, (((1,), (1,)), ((), ())), preferred_element_type=jnp.float32)
-        scores = scores + bias[...]
-        top = jnp.max(scores, axis=1, keepdims=True)
-        weights = jnp.exp2((scores - top) * scale)
+        return scores + bias[...]
+
+    expanded = [expand(n) for n in range(heads)]
+    scores = [score(query_of(n), expanded[n]) for n in range(heads)]
+    for n in range(heads):
+        top = jnp.max(scores[n], axis=1, keepdims=True)
+        weights = jnp.exp2((scores[n] - top) * scale)
         total = jnp.sum(weights, axis=1, keepdims=True)
-        mixed = jnp.dot(weights.astype(jnp.bfloat16), expanded[:, ND:], preferred_element_type=jnp.float32)
+        mixed = jnp.dot(weights.astype(jnp.bfloat16), expanded[n][:, ND:], preferred_element_type=jnp.float32)
         out_ref[:, n * VD : (n + 1) * VD] = (mixed / total).astype(jnp.bfloat16)
 
 
@@ -231,7 +240,7 @@
             grid=(all_heads // heads,),
             in_specs=[
                 whole((tok, ql)),
-                whole((1, ql)),
+                pl.BlockSpec((ql,), lambda i, *refs: (0,)),
                 whole((keys, width)),
                 whole((1, KL)),
                 pl.BlockSpec((ql, heads * (ND + RD)), lambda i, *refs: (0, i)),
@@ -261,7 +270,7 @@
         q_rows, window = gather(q_latent, kv_cache, nc, nh)
         first = (lax.axis_index("ctx") * q_rows.shape[0]).astype(jnp.int32).reshape(1)
         window = window.reshape(-1, window.shape[-1])
-        return attend(first, doc_lengths, q_rows, q_gain[None], window, kv_gain[None], w_query, w_kv, 4)
+        return attend(first, doc_lengths, q_rows, q_gain, window, kv_gain[None], w_query, w_kv, 4)
 
     placed = (
         P(("ctx", "head"), None),

time: 67.4 us -> 50.8 us (0.75)
  Pallas kernels: 65.9 us -> 50.7 us
  local copies, waits for them, and re-layouts: 1.29 us -> 0 us
    pallas_call x1, Pallas kernels: 44 us -> 28.8 us  [attend(): pl.pallas_call(functools.partial(attend_kernel, heads), out_shape=jax.Sha...]
    broadcast_in_dim x1 -> x0, local copies, waits for them, and re-layouts: 1.29 us -> none  [body(): q_gain[None]]
where the time goes in v2:
time: 50.8 us; the launch traced here: 50.7 us
  Pallas kernels  50.7 us (100%)
    pallas_call x1, Pallas kernels, attend(): pl.pallas_call(functools.partial(attend_kernel, heads), out_shape=jax.Sha...  28.8 us
    pallas_call x1, Pallas kernels, gather(): pl.pallas_call(functools.partial(gather_kernel, nc, nh), out_shape=(jax.S...  21.9 us

profile of v2, /device:TPU:25, one launch (start us, length us, event | category | flops | bytes accessed | tf_op | source)
XLA Modules:
  0.0 50.7 jit_solution(5478840288909928719)
XLA Ops:
  0.0 21.9 %gather.1 = (bf16[128,1536]{1,0:T(8,128)(2,1)}, bf16[9,128,576]{2,1,0:T(8,128)(2,1)}) custom-call(bf16[64,1536]{1,0:T(8,128)(2,1)} %q_ref.1, bf16[64,576]{1,0:T(8,128)(2,1)} %kv_ref.1), custom_call_target="tpu_custom_call" | custom-call | tf_op jit(solution)/shard_map/gather/pallas_call | solution.py:143
  21.9 28.8 %attend.1 = bf16[128,4096]{1,0:T(8,128)(2,1)} custom-call(s32[1]{0:T(128)} %bitcast.first_ref, s32[3]{0:T(128)} %len_ref.1, bf16[128,1536]{1,0:T(8,128)(2,1)} %get-tuple-element.7.q_ref, f32[1536]{0:T(1024)} %qg_ref.1, bf16[1152,576]{1,0:T(8,128)(2,1)} %bitcast.3, f32[1,512]{1,0:T(1,128)} %bitcast.4, bf16[1536,6144]{1,0:T(8,128)(2,1)} %wq_ref.1, ...), custom_call_target="tpu_custom_call" | custom-call | tf_op jit(solution)/shard_map/attend/pallas_call | solution.py:235
